TPU v7x, 32 devices: a whole 2x2x4 slice. The times are simulated.
32 devices in a mesh: ctx: 8 (over z, y), exp: 4 (over x, core).
Axes of the slice: x: 2, y: 2, z: 4, core: 2. Of those that a mesh axis runs over, the one named last changes fastest.
Arguments:
- queries: bfloat16 [1024, 4096], P('ctx', 'exp'), may hold values from -0.5 to 0.5
- attn_keys: bfloat16 [1024, 4096], P('ctx', 'exp'), may hold values from -0.5 to 0.5
- attn_values: bfloat16 [1024, 4096], P('ctx', 'exp'), may hold values from -3 to 3
- out_grad: bfloat16 [1024, 4096], P('ctx', 'exp'), may hold values from -0.75 to 0.75
- log_decay: float32 [1024, 32], P('ctx', 'exp'), may hold values from -1 to 0
- moe_input: bfloat16 [1024, 3072], P(('ctx', 'exp')), may hold values from -6 to 6
- routes: int32 [1024, 2], P(('ctx', 'exp')), may hold values from 0 to 7, all different within a row; in each aligned block of 32 rows (0 to 31, 32 to 63, ...) at most 16 rows name the same one
- route_weight: float32 [1024, 2], P(('ctx', 'exp')), may hold values from 0.25 to 1
- w_gate: bfloat16 [8, 9216, 3072], P('exp', 'ctx'), may hold values from -0.109375 to 0.109375
- w_up: bfloat16 [8, 9216, 3072], P('exp', 'ctx'), may hold values from -0.109375 to 0.109375
- w_down: bfloat16 [8, 9216, 3072], P('exp', 'ctx'), may hold values from -0.0625 to 0.0625
Outputs:
- attn_out: bfloat16 [1024, 4096], P('ctx', 'exp')
- grad_q: bfloat16 [1024, 4096], P('ctx', 'exp')
- grad_k: bfloat16 [1024, 4096], P('ctx', 'exp')
- derivative_wrt_entries: bfloat16 [1024, 4096], P('ctx', 'exp')
- moe_out: bfloat16 [1024, 3072], P(('ctx', 'exp'))
Inputs may be any that keep to these rules, and one draw needn't show every extreme that they name: `routes`: in the rows of one device no expert is named more than 16 times; each row names two different experts.
All inputs are finite; a program needn't handle non-finite values.
Results may differ from a plain program's by a relative error of at most 0.025.
Values may be sent and summed in bfloat16 or wider, within the bound.
No kernel may reach another device: no remote copies, remote signals or barrier semaphores. Data moves between devices by JAX's collectives and lax.ppermute only.
A program may use at most 128 MiB of HBM per device.

v0:
```python
import jax
import jax.numpy as jnp
from jax import lax
from jax.sharding import PartitionSpec as P


def entering(value, axis, combine, identity, reverse):
    length, position = (lax.axis_size(axis), lax.axis_index(axis))
    everything = jax.tree.map(
        lambda part, kind: lax.all_gather(part.astype(kind), axis),
        value,
        (jnp.bfloat16, jnp.bfloat16),
    )
    start = jax.tree.map(
        lambda part, zero: jnp.broadcast_to(jnp.asarray(zero, part.dtype), part.shape),
        value,
        identity,
    )

    def step(k, before):
        at = length - 1 - k if reverse else k
        reached = at > position if reverse else at < position
        new = combine(
            before, jax.tree.map(lambda part, own: part[at].astype(own.dtype), everything, value)
        )
        return jax.tree.map(lambda a, b: jnp.where(reached, a, b), new, before)

    return lax.fori_loop(0, length, step, start)


def chain_combine(earlier, later):
    return (earlier[0] * later[0], later[0][:, None, None] * earlier[1] + later[1])


def attention(queries, attn_keys, attn_values, out_grad, log_decay):
    length = queries.shape[0]
    heads = log_decay.shape[1]
    width = queries.shape[1] // heads
    shaped = (length, heads, width)
    q_heads = queries.reshape(shaped)
    k_heads = attn_keys.reshape(shaped)
    v_heads = attn_values.reshape(shaped)
    gradient_heads = out_grad.reshape(shaped)
    cum_decay = jnp.cumsum(log_decay, axis=0)
    total = cum_decay[length - 1]
    position = jnp.arange(length, dtype=jnp.int32)
    causal = (position[:, None] >= position[None, :])[None]
    spread = cum_decay.T[:, :, None] - cum_decay.T[:, None, :]
    block_weight = jnp.where(causal, jnp.exp(jnp.where(causal, spread, 0.0)), 0.0)
    rising_edge = jnp.exp(cum_decay)[:, :, None]
    falling_edge = jnp.exp(total[None, :] - cum_decay)[:, :, None]
    scaled_queries = q_heads.astype(jnp.float32) * rising_edge
    full_keys = k_heads.astype(jnp.float32)
    full_values = v_heads.astype(jnp.float32)
    scaled_gradient = gradient_heads.astype(jnp.float32) * rising_edge
    running_block_state = jnp.einsum(
        "mly,mlf->lyf", full_keys * falling_edge, full_values, precision=lax.Precision.HIGHEST
    )
    state_gradient = jnp.einsum(
        "nbd,nbw->bdw",
        scaled_queries,
        gradient_heads.astype(jnp.float32),
        precision=lax.Precision.HIGHEST,
    )
    growth = jnp.exp(total)
    identity = (jnp.ones((heads,), jnp.float32), jnp.zeros((heads, width, width), jnp.float32))
    prior_memory_matrix = entering(
        (growth, running_block_state), "ctx", chain_combine, identity, False
    )[1]
    following_state = entering((growth, state_gradient), "ctx", chain_combine, identity, True)[1]
    scores = jnp.einsum("thd,shd->hts", q_heads, k_heads, preferred_element_type=jnp.float32)
    attention_result = (scores * block_weight).astype(jnp.bfloat16)
    layer_output = jnp.einsum(
        "pgm,mpo->gpo", attention_result, v_heads, preferred_element_type=jnp.float32
    )
    layer_output = layer_output + jnp.einsum(
        "bip,ipu->biu", scaled_queries, prior_memory_matrix, precision=lax.Precision.HIGHEST
    )
    dscores = jnp.einsum(
        "thd,shd->hts", gradient_heads, v_heads, preferred_element_type=jnp.float32
    )
    weight_gradient = (dscores * block_weight).astype(jnp.bfloat16)
    query_gradient = jnp.einsum(
        "pgm,mpo->gpo", weight_gradient, k_heads, preferred_element_type=jnp.float32
    )
    query_gradient = query_gradient + jnp.einsum(
        "pig,ijg->pij", scaled_gradient, prior_memory_matrix, precision=lax.Precision.HIGHEST
    )
    key_gradient = jnp.einsum(
        "nkg,knv->gnv", weight_gradient, q_heads, preferred_element_type=jnp.float32
    )
    key_gradient = key_gradient + falling_edge * jnp.einsum(
        "jnr,nbr->jnb", full_values, following_state, precision=lax.Precision.HIGHEST
    )
    value_gradient = jnp.einsum(
        "nkg,knv->gnv", attention_result, gradient_heads, preferred_element_type=jnp.float32
    )
    value_gradient = value_gradient + falling_edge * jnp.einsum(
        "umj,mje->ume", full_keys, following_state, precision=lax.Precision.HIGHEST
    )
    flat_shape = (length, queries.shape[1])
    return (
        layer_output.reshape(flat_shape).astype(jnp.bfloat16),
        query_gradient.reshape(flat_shape).astype(jnp.bfloat16),
        key_gradient.reshape(flat_shape).astype(jnp.bfloat16),
        value_gradient.reshape(flat_shape).astype(jnp.bfloat16),
    )


def route_tables(routes, route_weight, experts, capacity):
    row_count = routes.shape[0]
    flat_routes = routes.reshape(row_count * 2)
    one_hot = (flat_routes[:, None] == jnp.arange(experts, dtype=jnp.int32)[None, :]).astype(
        jnp.int32
    )
    earlier_count = jnp.cumsum(one_hot, axis=0) - one_hot
    slot_index = jnp.sum(earlier_count * one_hot, axis=1)
    target = flat_routes * capacity + slot_index
    member = (jnp.arange(experts * capacity, dtype=jnp.int32)[:, None] == target[None, :]).astype(
        jnp.float32
    )
    picker = member.reshape(experts * capacity, row_count, 2).sum(axis=2)
    merge_lookup = (
        (member * route_weight.reshape(row_count * 2)[None, :])
        .reshape(experts * capacity, row_count, 2)
        .sum(axis=2)
    )
    return (picker, merge_lookup)


def expert_terms(piece, w_gate, w_up, w_down):
    outputs = []
    for local in range(w_gate.shape[0]):
        rows = piece[:, :, local].reshape(-1, piece.shape[-1])
        gate_value = jnp.einsum(
            "md,fd->mf", rows, w_gate[local], preferred_element_type=jnp.float32
        )
        up_value = jnp.einsum("md,fd->mf", rows, w_up[local], preferred_element_type=jnp.float32)
        hidden = (jax.nn.silu(gate_value) * up_value).astype(jnp.bfloat16)
        result = jnp.dot(hidden, w_down[local], preferred_element_type=jnp.float32)
        outputs.append(
            result.reshape(piece.shape[0], piece.shape[1], piece.shape[3], piece.shape[4])
        )
    return jnp.stack(outputs, axis=2)


def experts(moe_input, routes, route_weight, w_gate, w_up, w_down):
    groups = lax.axis_size("exp")
    local_count = w_gate.shape[0]
    row_total = moe_input.shape[0]
    capacity = max(2, row_total // 2)
    picker, merge_lookup = route_tables(routes, route_weight, groups * local_count, capacity)
    departing_memory = jnp.dot(
        picker.astype(jnp.bfloat16), moe_input, preferred_element_type=jnp.float32
    ).astype(jnp.bfloat16)
    departing_memory = departing_memory.reshape(groups, local_count, capacity, moe_input.shape[1])
    arrived = lax.all_to_all(departing_memory, "exp", split_axis=0, concat_axis=0, tiled=True)
    gathered = lax.all_gather(arrived[None], "ctx", axis=0, tiled=True)
    terms = expert_terms(gathered, w_gate, w_up, w_down)
    summed = lax.psum_scatter(
        terms.astype(jnp.bfloat16), "ctx", scatter_dimension=0, tiled=True
    ).astype(jnp.float32)
    finished = summed[0].astype(jnp.bfloat16)
    returned = lax.all_to_all(finished, "exp", split_axis=0, concat_axis=0, tiled=True)
    returned = returned.reshape(groups * local_count * capacity, moe_input.shape[1])
    mixed = jnp.dot(merge_lookup.T, returned.astype(jnp.float32), precision=lax.Precision.HIGHEST)
    return mixed.astype(jnp.bfloat16)


def body(
    queries,
    attn_keys,
    attn_values,
    out_grad,
    log_decay,
    moe_input,
    routes,
    route_weight,
    w_gate,
    w_up,
    w_down,
):
    attention_parts = attention(queries, attn_keys, attn_values, out_grad, log_decay)
    moe_out = experts(moe_input, routes, route_weight, w_gate, w_up, w_down)
    return attention_parts + (moe_out,)


def solution(mesh):
    placed = (
        P("ctx", "exp"),
        P("ctx", "exp"),
        P("ctx", "exp"),
        P("ctx", "exp"),
        P("ctx", "exp"),
        P(("ctx", "exp"), None),
        P(("ctx", "exp"), None),
        P(("ctx", "exp"), None),
        P("exp", "ctx", None),
        P("exp", "ctx", None),
        P("exp", "ctx", None),
    )
    return jax.shard_map(
        body,
        mesh=mesh,
        in_specs=placed,
        out_specs=(
            P("ctx", "exp"),
            P("ctx", "exp"),
            P("ctx", "exp"),
            P("ctx", "exp"),
            P(("ctx", "exp"), None),
        ),
        check_vma=False,
    )
```

profile of v0, /device:TPU:0, one launch (start us, length us, event | category | flops | bytes accessed | tf_op | source)
XLA Modules:
  0.0 465.3 jit_solution(8278910734743402851)
XLA Ops:
  10.2 1.3 convolution_convert_fusion
  11.5 15.8 %all_to_all.10 = bf16[4,2,16,3072]{3,2,1,0:T(8,128)(2,1)} all-to-all(bf16[4,2,16,3072]{3,2,1,0:T(8,128)(2,1)S(1)} %bitcast.199), channel_id=1, replica_groups=mesh['ctx'=8,'exp'=4] {'exp'}, dimensions={0} | all-to-all | bytes 1572864 | tf_op jit(solution)/shard_map/all_to_all | solution.py:157
  28.0 1.1 convolution_convert_fusion.3
  29.6 1.4 convolution_convert_fusion.2
  31.8 21.9 %all-gather.3 = bf16[8,1,8]{2,1,0:T(2,128)(2,1)S(1)} all-gather(bf16[1,1,8]{2,1,0:T(2,128)(2,1)S(1)} %get-tuple-element.321), channel_id=1, replica_groups=mesh['ctx'=8,'exp'=4] {'ctx'}, dimensions={0}, use_global_device_ids=true | all-gather | bytes 144 | tf_op jit(solution)/shard_map/all_gather | solution.py:10
  54.4 72.6 %all-gather.12.cloned.1.call-done = bf16[32,2,16,3072]{3,2,1,0:T(8,128)(2,1)} async-done(((bf16[4,2,16,3072]{3,2,1,0:T(8,128)(2,1)}), bf16[32,2,16,3072]{3,2,1,0:T(8,128)(2,1)}) %all-gather.12.cloned.1.call-update) | async-done | bytes 6291472 | tf_op jit(solution)/shard_map/all_gather | solution.py:158
  127.0 3.5 fusion.74
  130.5 8.7 %fusion.8 = f32[512,1152]{1,0:T(8,128)} fusion(bf16[512,3072]{1,0:T(8,128)(2,1)S(1)} %bitcast.202, bf16[2,1152,3072]{2,1,0:T(8,128)(2,1)} %param.23), kind=kOutput, calls=%fused_computation.12 | convolution fusion | flops 3623878656 | bytes 12582912 | tf_op jit(solution)/shard_map/md,fd->mf/dot_general | solution.py:135
  139.2 5.7 %fusion.12 = f32[512,1152]{1,0:T(8,128)} fusion(bf16[512,3072]{1,0:T(8,128)(2,1)S(1)} %bitcast.200, bf16[2,1152,3072]{2,1,0:T(8,128)(2,1)S(1)} %bitcast.213), kind=kOutput, calls=%fused_computation.16 | convolution fusion | flops 3623878656 | bytes 12582912 | tf_op jit(solution)/shard_map/md,fd->mf/dot_general | solution.py:135
  144.9 8.1 %fusion.38 = bf16[512,1152]{1,0:T(8,128)(2,1)S(1)} fusion(bf16[512,3072]{1,0:T(8,128)(2,1)S(1)} %bitcast.203, bf16[2,1152,3072]{2,1,0:T(8,128)(2,1)} %param.24, f32[512,1152]{1,0:T(8,128)} %fusion.8), kind=kOutput, calls=%fused_computation.33 | convolution fusion | flops 3627417600 | bytes 13762560 | tf_op jit(solution)/shard_map/md,fd->mf/dot_general | solution.py:138
  153.1 7.6 %fusion.41 = bf16[512,1152]{1,0:T(8,128)(2,1)S(1)} fusion(bf16[512,3072]{1,0:T(8,128)(2,1)S(1)} %bitcast.201, bf16[2,1152,3072]{2,1,0:T(8,128)(2,1)} %param.24, f32[512,1152]{1,0:T(8,128)S(1)} %copy-done.8), kind=kOutput, calls=%fused_computation.34 | convolution fusion | flops 3627417600 | bytes 13762560 | tf_op jit(solution)/shard_map/md,fd->mf/dot_general | solution.py:138
  160.6 7.6 %fusion.26 = bf16[8,4,1,16,3072]{4,3,1,0,2:T(8,128)(2,1)S(1)} fusion(bf16[8,4,16,1152]{3,2,1,0:T(8,128)(2,1)S(1)} %bitcast.214, bf16[2,1152,3072]{2,1,0:T(8,128)(2,1)} %param.25), kind=kOutput, calls=%fused_computation.27 | convolution fusion | flops 3625451520 | bytes 11403264 | tf_op jit(solution)/shard_map/dot_general | solution.py:140
  168.3 7.8 %fusion.29 = bf16[8,4,1,16,3072]{4,3,1,0,2:T(8,128)(2,1)S(1)} fusion(bf16[8,4,16,1152]{3,2,1,0:T(8,128)(2,1)S(1)} %bitcast.215, bf16[2,1152,3072]{2,1,0:T(8,128)(2,1)} %param.25), kind=kOutput, calls=%fused_computation.28 | convolution fusion | flops 3625451520 | bytes 11403264 | tf_op jit(solution)/shard_map/dot_general | solution.py:140
  176.0 3.2 pad_maximum_fusion
  179.2 9.1 %while.30 = (s32[]{:T(128)}, f32[8,128,128]{2,1,0:T(8,128)S(1)}, s32[]{:T(128)}, bf16[8,8]{1,0:T(8,128)(2,1)S(1)}, bf16[8,8,128,128]{3,2,1,0:T(8,128)(2,1)}, /*index=5*/s32[]{:T(128)}, s32[]{:T(128)}) while((s32[]{:T(128)}, f32[8,128,128]{2,1,0:T(8,128)S(1)}, s32[]{:T(128)}, bf16[8,8]{1,0:T(8,128)(2,1)S(1)}, ...), condition=%wide.region_2.3_spmd.clone, body=%wide.region_1.2_spmd.clone.sunk | while | flops 655372 | bytes 1310913 | solution.py:28
  179.3 1.1 fusion.108
  180.4 1.1 fusion.108
  181.5 1.1 fusion.108
  185.0 1.1 fusion.108
  186.1 1.1 fusion.108
  187.2 1.1 fusion.108
  190.0 37.3 %all-gather.10.cloned.1.call-done = bf16[64,128,128]{2,1,0:T(8,128)(2,1)} async-done(((bf16[8,128,128]{2,1,0:T(8,128)(2,1)}), bf16[64,128,128]{2,1,0:T(8,128)(2,1)}) %all-gather.10.cloned.1.call-update) | async-done | bytes 2097168 | tf_op jit(solution)/shard_map/all_gather | solution.py:10
  227.3 9.2 %while.31 = (s32[]{:T(128)}, f32[8,128,128]{2,1,0:T(8,128)S(1)}, s32[]{:T(128)}, bf16[8,8]{1,0:T(8,128)(2,1)S(1)}, bf16[8,8,128,128]{3,2,1,0:T(8,128)(2,1)}, /*index=5*/s32[]{:T(128)}, s32[]{:T(128)}, s32[]{:T(128)}, s32[]{:T(128)}) while((s32[]{:T(128)}, f32[8,128,128]{2,1,0:T(8,128)S(1)}, s32[]{:T(128)}, ...), condition=%wide.region_4.5_spmd.clone, body=%wide.region_3.4_spmd.clone.sunk | while | flops 655376 | bytes 1310975 | solution.py:28
  228.5 1.1 fusion.109
  234.2 1.2 fusion.109
  235.4 1.1 fusion.109
  239.2 200.7 %all-reduce.3.cloned.1.call-done = bf16[8,4,2,16,3072]{4,3,1,0,2:T(8,128)(2,1)} async-done(((bf16[8,4,2,16,3072]{4,3,1,0,2:T(8,128)(2,1)}), bf16[8,4,2,16,3072]{4,3,1,0,2:T(8,128)(2,1)}) %all-reduce.3.cloned.1.call-update) | async-done | bytes 6291472
  439.8 1.8 dynamic-slice_bitcast_fusion
  442.6 3.5 all-to-all-start.1
  447.2 1.8 copy.169
  452.3 5.4 %all-to-all-done.1 = bf16[4,2,16,3072]{3,2,1,0:T(8,128)(2,1)S(1)} async-done(((bf16[4,2,16,3072]{3,2,1,0:T(8,128)(2,1)}), bf16[4,2,16,3072]{3,2,1,0:T(8,128)(2,1)S(1)}, u32[]{:S(2)}, u32[]{:S(2)}) %all-to-all-start.1) | async-done | bytes 786464 | tf_op jit(solution)/shard_map/all_to_all | solution.py:164
  457.7 1.1 convolution_convert_fusion.1
  (97 shorter events, 22.9 us)
Async XLA Ops:
  7.2 20.8 %copy-start = (bf16[128,1024]{1,0:T(8,128)(2,1)S(1)}, bf16[128,1024]{1,0:T(8,128)(2,1)}, u32[]{:S(2)}) copy-start(bf16[128,1024]{1,0:T(8,128)(2,1)} %param.17) | copy-start | bytes 786436
  7.2 20.2 %copy-start.6 = (f32[128,8]{0,1:T(8,128)S(1)}, f32[128,8]{0,1:T(8,128)}, u32[]{:S(2)}) copy-start(f32[128,8]{0,1:T(8,128)} %param.19) | copy-start | bytes 12292
  7.2 20.3 %copy-start.3 = (bf16[128,1024]{1,0:T(8,128)(2,1)S(1)}, bf16[128,1024]{1,0:T(8,128)(2,1)}, u32[]{:S(2)}) copy-start(bf16[128,1024]{1,0:T(8,128)(2,1)} %param.16) | copy-start | bytes 786436
  7.2 22.0 %copy-start.4 = (bf16[128,1024]{1,0:T(8,128)(2,1)S(1)}, bf16[128,1024]{1,0:T(8,128)(2,1)}, u32[]{:S(2)}) copy-start(bf16[128,1024]{1,0:T(8,128)(2,1)} %param.15) | copy-start | bytes 786436
  7.2 22.2 %copy-start.5 = (bf16[128,1024]{1,0:T(8,128)(2,1)S(1)}, bf16[128,1024]{1,0:T(8,128)(2,1)}, u32[]{:S(2)}) copy-start(bf16[128,1024]{1,0:T(8,128)(2,1)} %param.18) | copy-start | bytes 786436
  7.2 119.8 %all-gather.12.cloned.1.call-start = ((), (), s32[]{:S(2)}) async-start(), calls=%async_computation.4 | async-start | bytes 7077888 | tf_op jit(solution)/shard_map/all_gather | solution.py:158
  27.3 151.9 %all-gather.8.cloned.1.call-start = ((), (), s32[]{:S(2)}) async-start(), calls=%async_computation.2 | async-start | bytes 2359296 | tf_op jit(solution)/shard_map/all_gather | solution.py:10
  27.9 25.9 %copy-start.7 = (u32[32]{0:T(128)S(1)}, u32[32]{0:T(128)}, u32[]{:S(2)}) copy-start(u32[32]{0:T(128)} %constant.94) | copy-start | bytes 388
  29.1 198.2 %all-gather.10.cloned.1.call-start = ((), (), s32[]{:S(2)}) async-start(), calls=%async_computation.3 | async-start | bytes 2359296 | tf_op jit(solution)/shard_map/all_gather | solution.py:10
  31.0 408.8 %all-reduce.3.cloned.1.call-start = ((), (), s32[]{:S(2)}) async-start(), calls=%async_computation.5 | async-start | bytes 12582912
  127.0 12.2 %slice-start = ((s8[14155776]{0:T(1024)(128)(4,1)}), s8[4194304]{0:T(1024)(128)(4,1)S(1)}, s32[]{:S(2)}) async-start(s8[14155776]{0:T(1024)(128)(4,1)} %bitcast.212), calls=%async_computation.6 | async-start | bytes 8388608
  127.0 12.2 %slice-start.1 = ((s8[14155776]{0:T(1024)(128)(4,1)}), s8[4194304]{0:T(1024)(128)(4,1)S(1)}, s32[]{:S(2)}) async-start(s8[14155776]{0:T(1024)(128)(4,1)} %bitcast.212), calls=%async_computation.7 | async-start | bytes 8388608
  130.5 8.7 %slice-start.2 = ((s8[14155776]{0:T(1024)(128)(4,1)}), s8[4194304]{0:T(1024)(128)(4,1)S(1)}, s32[]{:S(2)}) async-start(s8[14155776]{0:T(1024)(128)(4,1)} %bitcast.212), calls=%async_computation.8 | async-start | bytes 8388608
  130.5 8.7 %slice-start.3 = ((s8[14155776]{0:T(1024)(128)(4,1)}), s8[1572864]{0:T(1024)(128)(4,1)S(1)}, s32[]{:S(2)}) async-start(s8[14155776]{0:T(1024)(128)(4,1)} %bitcast.212), calls=%async_computation.9 | async-start | bytes 3145728
  144.9 8.1 %copy-start.8 = (f32[512,1152]{1,0:T(8,128)S(1)}, f32[512,1152]{1,0:T(8,128)}, u32[]{:S(2)}) copy-start(f32[512,1152]{1,0:T(8,128)} %fusion.12) | copy-start | bytes 7077892
  439.8 9.1 %copy-start.1 = (bf16[128,8,128]{0,2,1:T(8,128)(2,1)S(1)}, bf16[128,8,128]{0,2,1:T(8,128)(2,1)}, u32[]{:S(2)}) copy-start(bf16[128,8,128]{0,2,1:T(8,128)(2,1)} %fusion.54) | copy-start | bytes 786436
  441.6 8.2 %copy-start.2 = (bf16[128,8,128]{0,2,1:T(8,128)(2,1)S(1)}, bf16[128,8,128]{0,2,1:T(8,128)(2,1)}, u32[]{:S(2)}) copy-start(bf16[128,8,128]{0,2,1:T(8,128)(2,1)} %fusion.53) | copy-start | bytes 786436
  442.6 15.1 %all-to-all-start.1 = ((bf16[4,2,16,3072]{3,2,1,0:T(8,128)(2,1)}), bf16[4,2,16,3072]{3,2,1,0:T(8,128)(2,1)S(1)}, u32[]{:S(2)}, u32[]{:S(2)}) async-start(bf16[4,2,16,3072]{3,2,1,0:T(8,128)(2,1)} %copy.168), calls=%async_computation.1 | async-start | bytes 1572864 | tf_op jit(solution)/shard_map/all_to_all | solution.py:164
Sparse Core Ops, SparseCore 0:
  27.4 99.4 all-gather.11
  129.7 47.2 all-gather.7
  179.7 47.5 all-gather.9
  231.0 208.8 all-reduce.2
where the time goes:
time: 466 us; the launch traced here: 465 us
  waiting for transfers between devices  316 us (68%)
  matrix products  57.2 us (12%)
  blocking collectives  37.7 us (8%)
  other arithmetic  22.9 us (5%)
  between operations  14.1 us (3%)
  local copies, waits for them, and re-layouts  13.2 us (3%)
    unnamed x5, waiting for transfers between devices  201 us
    all_gather x1, waiting for transfers between devices, experts(): gathered = lax.all_gather(arrived[None], 'ctx', axis=0, tiled=True)  72.6 us
    all_gather x2, waiting for transfers between devices, entering(): lax.all_gather(part.astype(kind), axis)  37.3 us
    all_gather x1, blocking collectives, entering(): lax.all_gather(part.astype(kind), axis)  21.9 us
    select_n x16, other arithmetic, step(): return jax.tree.map(lambda a, b: jnp.where(reached, a, b), new, before)  17.6 us
    all_to_all x1, blocking collectives, experts(): lax.all_to_all(departing_memory, 'exp', split_axis=0, concat_axis=0, tile...  15.8 us
    dot_general x2, matrix products, expert_terms(): jnp.einsum('md,fd->mf', rows, w_up[local], preferred_element_type=jnp.flo...  15.7 us
    dot_general x2, matrix products, expert_terms(): result = jnp.dot(hidden, w_down[local], preferred_element_type=jnp.float32)  15.4 us
  transfers between devices with their start and end apart: 5, of which 4 were waited for; matrix products, arithmetic and copies ran while one was open for 18% of the time, Pallas kernels for 0%

commit v1 on v0

--- a/solution.py
+++ b/solution.py
@@ -155,7 +155,12 @@
     ).astype(jnp.bfloat16)
     departing_memory = departing_memory.reshape(groups, local_count, capacity, moe_input.shape[1])
     arrived = lax.all_to_all(departing_memory, "exp", split_axis=0, concat_axis=0, tiled=True)
-    gathered = lax.all_gather(arrived[None], "ctx", axis=0, tiled=True)
+    ring = [arrived[None]]
+    for hop in range(7):
+        ring.append(lax.ppermute(ring[-1], "ctx", [(dev, (dev + 1) % 8) for dev in range(8)]))
+    gathered = jnp.roll(
+        jnp.concatenate(ring[::-1], axis=0), (lax.axis_index("ctx") + 1) * ring[0].shape[0], axis=0
+    )
     terms = expert_terms(gathered, w_gate, w_up, w_down)
     summed = lax.psum_scatter(
         terms.astype(jnp.bfloat16), "ctx", scatter_dimension=0, tiled=True

time: 466 us -> 486 us (1.043)
  local copies, waits for them, and re-layouts: 13.2 us -> 24 us
  waiting for transfers between devices: 316 us -> 326 us
    ppermute x0 -> x7, waiting for transfers between devices: none -> 134 us  [experts(): lax.ppermute(ring[-1], 'ctx', [(dev, (dev + 1) % 8) for dev in range(8)])]
    all_gather x1 -> x0, waiting for transfers between devices: 72.6 us -> none  [experts(): gathered = lax.all_gather(arrived[None], 'ctx', axis=0, tiled=True)]
    all_gather x2, waiting for transfers between devices: 37.3 us -> 0.02 us  [entering(): lax.all_gather(part.astype(kind), axis)]
    unnamed x5 -> x4, waiting for transfers between devices: 201 us -> 186 us
    unnamed x35 -> x46, local copies, waits for them, and re-layouts: 6.1 us -> 17.4 us
  transfers between devices with their start and end apart: 5 -> 11, of which waited for: 4 -> 8; matrix products, arithmetic and copies ran while one was open for 18% -> 19% of each run, Pallas kernels for 0% -> 0%
where the time goes in v1:
time: 486 us; the launch traced here: 485 us
  waiting for transfers between devices  326 us (67%)
  matrix products  54 us (11%)
  blocking collectives  38.7 us (8%)
  local copies, waits for them, and re-layouts  24 us (5%)
  other arithmetic  22.8 us (5%)
  between operations  14.2 us (3%)
  starting transfers between devices  5.14 us (1%)
    unnamed x4, waiting for transfers between devices  186 us
    ppermute x7, waiting for transfers between devices, experts(): lax.ppermute(ring[-1], 'ctx', [(dev, (dev + 1) % 8) for dev in range(8)])  134 us
    all_gather x1, blocking collectives, entering(): lax.all_gather(part.astype(kind), axis)  23 us
    select_n x16, other arithmetic, step(): return jax.tree.map(lambda a, b: jnp.where(reached, a, b), new, before)  17.5 us
    unnamed x46, local copies, waits for them, and re-layouts  17.4 us
    all_to_all x1, blocking collectives, experts(): lax.all_to_all(departing_memory, 'exp', split_axis=0, concat_axis=0, tile...  15.7 us
    dot_general x2, matrix products, expert_terms(): result = jnp.dot(hidden, w_down[local], preferred_element_type=jnp.float32)  15.3 us
    dot_general x2, matrix products, expert_terms(): jnp.einsum('md,fd->mf', rows, w_up[local], preferred_element_type=jnp.flo...  14.6 us
  transfers between devices with their start and end apart: 11, of which 8 were waited for; matrix products, arithmetic and copies ran while one was open for 19% of the time, Pallas kernels for 0%

profile of v1, /device:TPU:0, one launch (start us, length us, event | category | flops | bytes accessed | tf_op | source)
XLA Modules:
  0.0 485.1 jit_solution(6574316420265048099)
XLA Ops:
  10.1 1.3 convolution_convert_fusion
  11.5 15.7 %all_to_all.10 = bf16[4,2,16,3072]{3,2,1,0:T(8,128)(2,1)S(1)} all-to-all(bf16[4,2,16,3072]{3,2,1,0:T(8,128)(2,1)S(1)} %bitcast.201), channel_id=1, replica_groups=mesh['ctx'=8,'exp'=4] {'exp'}, dimensions={0} | all-to-all | bytes 1572864 | tf_op jit(solution)/shard_map/all_to_all | solution.py:157
  27.1 1.5 collective-permute-start
  29.6 19.3 %collective-permute-done = bf16[1,4,2,16,3072]{4,3,2,1,0:T(8,128)(2,1)S(1)} collective-permute-done((bf16[1,4,2,16,3072]{4,3,2,1,0:T(8,128)(2,1)S(1)}, bf16[1,4,2,16,3072]{4,3,2,1,0:T(8,128)(2,1)S(1)}, u32[]{:S(2)}, u32[]{:S(2)}) %collective-permute-start) | collective-permute-done | bytes 786464 | tf_op jit(solution)/shard_map/ppermute | solution.py:160
  49.0 1.3 copy.184
  51.4 1.4 convolution_convert_fusion.2
  52.9 22.1 %collective-permute-done.1 = bf16[1,4,2,16,3072]{4,3,2,1,0:T(8,128)(2,1)S(1)} collective-permute-done((bf16[1,4,2,16,3072]{4,3,2,1,0:T(8,128)(2,1)S(1)}, bf16[1,4,2,16,3072]{4,3,2,1,0:T(8,128)(2,1)S(1)}, u32[]{:S(2)}, u32[]{:S(2)}) %collective-permute-start.1) | collective-permute-done | bytes 786464 | tf_op jit(solution)/shard_map/ppermute | solution.py:160
  75.0 20.0 %collective-permute-done.2 = bf16[1,4,2,16,3072]{4,3,2,1,0:T(8,128)(2,1)S(1)} collective-permute-done((bf16[1,4,2,16,3072]{4,3,2,1,0:T(8,128)(2,1)S(1)}, bf16[1,4,2,16,3072]{4,3,2,1,0:T(8,128)(2,1)S(1)}, u32[]{:S(2)}, u32[]{:S(2)}) %collective-permute-start.2) | collective-permute-done | bytes 786464 | tf_op jit(solution)/shard_map/ppermute | solution.py:160
  95.9 37.2 %collective-permute-done.3 = bf16[1,4,2,16,3072]{4,3,2,1,0:T(8,128)(2,1)S(1)} collective-permute-done((bf16[1,4,2,16,3072]{4,3,2,1,0:T(8,128)(2,1)S(1)}, bf16[1,4,2,16,3072]{4,3,2,1,0:T(8,128)(2,1)S(1)}, u32[]{:S(2)}, u32[]{:S(2)}) %collective-permute-start.3) | collective-permute-done | bytes 786464 | tf_op jit(solution)/shard_map/ppermute | solution.py:160
  134.0 17.5 %collective-permute-done.4 = bf16[1,4,2,16,3072]{4,3,2,1,0:T(8,128)(2,1)} collective-permute-done((bf16[1,4,2,16,3072]{4,3,2,1,0:T(8,128)(2,1)S(1)}, bf16[1,4,2,16,3072]{4,3,2,1,0:T(8,128)(2,1)}, u32[]{:S(2)}, u32[]{:S(2)}) %collective-permute-start.4) | collective-permute-done | bytes 786464 | tf_op jit(solution)/shard_map/ppermute | solution.py:160
  152.7 17.5 %collective-permute-done.5 = bf16[1,4,2,16,3072]{4,3,2,1,0:T(8,128)(2,1)} collective-permute-done((bf16[1,4,2,16,3072]{4,3,2,1,0:T(8,128)(2,1)}, bf16[1,4,2,16,3072]{4,3,2,1,0:T(8,128)(2,1)}, u32[]{:S(2)}, u32[]{:S(2)}) %collective-permute-start.5) | collective-permute-done | bytes 786464 | tf_op jit(solution)/shard_map/ppermute | solution.py:160
  171.4 23.0 %all-gather.2 = bf16[8,1,8]{2,1,0:T(2,128)(2,1)S(1)} all-gather(bf16[1,1,8]{2,1,0:T(2,128)(2,1)S(1)} %get-tuple-element.321), channel_id=1, replica_groups=mesh['ctx'=8,'exp'=4] {'ctx'}, dimensions={0}, use_global_device_ids=true | all-gather | bytes 144 | tf_op jit(solution)/shard_map/all_gather | solution.py:10
  195.9 1.2 constant_dynamic-update-slice_fusion.15
  197.1 1.2 constant_dynamic-update-slice_fusion.14
  198.3 1.4 constant_dynamic-update-slice_fusion.13
  200.0 1.2 constant_dynamic-update-slice_fusion.7
  201.2 1.2 constant_dynamic-update-slice_fusion.6
  202.4 1.2 constant_dynamic-update-slice_fusion.5
  204.7 6.7 %fusion.12 = f32[512,1152]{1,0:T(8,128)S(1)} fusion(bf16[512,3072]{1,0:T(8,128)(2,1)S(1)} %bitcast.204, bf16[2,1152,3072]{2,1,0:T(8,128)(2,1)} %param.23), kind=kOutput, calls=%fused_computation.16 | convolution fusion | flops 3623878656 | bytes 12582912 | tf_op jit(solution)/shard_map/md,fd->mf/dot_general | solution.py:135
  211.4 6.5 %fusion.8 = f32[512,1152]{1,0:T(8,128)S(1)} fusion(bf16[512,3072]{1,0:T(8,128)(2,1)S(1)} %bitcast.202, bf16[2,1152,3072]{2,1,0:T(8,128)(2,1)} %param.23), kind=kOutput, calls=%fused_computation.12 | convolution fusion | flops 3623878656 | bytes 12582912 | tf_op jit(solution)/shard_map/md,fd->mf/dot_general | solution.py:135
  218.0 7.3 %fusion.41 = bf16[512,1152]{1,0:T(8,128)(2,1)S(1)} fusion(bf16[512,3072]{1,0:T(8,128)(2,1)S(1)} %bitcast.205, bf16[2,1152,3072]{2,1,0:T(8,128)(2,1)} %param.24, f32[512,1152]{1,0:T(8,128)S(1)} %fusion.12), kind=kOutput, calls=%fused_computation.34 | convolution fusion | flops 3627417600 | bytes 13762560 | tf_op jit(solution)/shard_map/md,fd->mf/dot_general | solution.py:138
  225.3 7.3 %fusion.38 = bf16[512,1152]{1,0:T(8,128)(2,1)S(1)} fusion(bf16[512,3072]{1,0:T(8,128)(2,1)S(1)} %bitcast.203, bf16[2,1152,3072]{2,1,0:T(8,128)(2,1)} %param.24, f32[512,1152]{1,0:T(8,128)S(1)} %fusion.8), kind=kOutput, calls=%fused_computation.33 | convolution fusion | flops 3627417600 | bytes 13762560 | tf_op jit(solution)/shard_map/md,fd->mf/dot_general | solution.py:138
  232.6 7.6 %fusion.29 = bf16[8,4,1,16,3072]{4,3,1,0,2:T(8,128)(2,1)S(1)} fusion(bf16[8,4,16,1152]{3,2,1,0:T(8,128)(2,1)S(1)} %bitcast.214, bf16[2,1152,3072]{2,1,0:T(8,128)(2,1)} %param.25), kind=kOutput, calls=%fused_computation.28 | convolution fusion | flops 3625451520 | bytes 11403264 | tf_op jit(solution)/shard_map/dot_general | solution.py:140
  240.2 7.7 %fusion.26 = bf16[8,4,1,16,3072]{4,3,1,0,2:T(8,128)(2,1)S(1)} fusion(bf16[8,4,16,1152]{3,2,1,0:T(8,128)(2,1)S(1)} %bitcast.215, bf16[2,1152,3072]{2,1,0:T(8,128)(2,1)} %param.25), kind=kOutput, calls=%fused_computation.27 | convolution fusion | flops 3625451520 | bytes 11403264 | tf_op jit(solution)/shard_map/dot_general | solution.py:140
  247.9 3.2 pad_maximum_fusion
  251.1 9.2 %while.31 = (s32[]{:T(128)}, f32[8,128,128]{2,1,0:T(8,128)S(1)}, s32[]{:T(128)}, bf16[8,8]{1,0:T(8,128)(2,1)S(1)}, bf16[8,8,128,128]{3,2,1,0:T(8,128)(2,1)}, /*index=5*/s32[]{:T(128)}, s32[]{:T(128)}, s32[]{:T(128)}, s32[]{:T(128)}) while((s32[]{:T(128)}, f32[8,128,128]{2,1,0:T(8,128)S(1)}, s32[]{:T(128)}, ...), condition=%wide.region_4.5_spmd.clone, body=%wide.region_3.4_spmd.clone.sunk | while | flops 655376 | bytes 1310967 | solution.py:28
  261.9 9.0 %while.30 = (s32[]{:T(128)}, f32[8,128,128]{2,1,0:T(8,128)S(1)}, s32[]{:T(128)}, bf16[8,8]{1,0:T(8,128)(2,1)S(1)}, bf16[8,8,128,128]{3,2,1,0:T(8,128)(2,1)}, /*index=5*/s32[]{:T(128)}, s32[]{:T(128)}) while((s32[]{:T(128)}, f32[8,128,128]{2,1,0:T(8,128)S(1)}, s32[]{:T(128)}, bf16[8,8]{1,0:T(8,128)(2,1)S(1)}, ...), condition=%wide.region_2.3_spmd.clone, body=%wide.region_1.2_spmd.clone.sunk | while | flops 655372 | bytes 1310905 | solution.py:28
  273.2 186.3 %all-reduce.3.cloned.1.call-done = bf16[8,4,2,16,3072]{4,3,1,0,2:T(8,128)(2,1)} async-done(((bf16[8,4,2,16,3072]{4,3,1,0,2:T(8,128)(2,1)}), bf16[8,4,2,16,3072]{4,3,1,0,2:T(8,128)(2,1)}) %all-reduce.3.cloned.1.call-update) | async-done | bytes 6291472
  459.5 1.9 dynamic-slice_bitcast_fusion
  462.3 3.5 all-to-all-start.1
  466.9 1.8 copy.171
  471.7 5.7 %all-to-all-done.1 = bf16[4,2,16,3072]{3,2,1,0:T(8,128)(2,1)S(1)} async-done(((bf16[4,2,16,3072]{3,2,1,0:T(8,128)(2,1)}), bf16[4,2,16,3072]{3,2,1,0:T(8,128)(2,1)S(1)}, u32[]{:S(2)}, u32[]{:S(2)}) %all-to-all-start.1) | async-done | bytes 786464 | tf_op jit(solution)/shard_map/all_to_all | solution.py:169
  (119 shorter events, 39.8 us)
Async XLA Ops:
  7.2 163.0 %copy-start = (bf16[128,1024]{1,0:T(8,128)(2,1)S(1)}, bf16[128,1024]{1,0:T(8,128)(2,1)}, u32[]{:S(2)}) copy-start(bf16[128,1024]{1,0:T(8,128)(2,1)} %param.17) | copy-start | bytes 786436
  7.2 187.3 %copy-start.10 = (u32[32]{0:T(128)S(1)}, u32[32]{0:T(128)}, u32[]{:S(2)}) copy-start(u32[32]{0:T(128)} %constant.117) | copy-start | bytes 388
  7.2 243.9 %all-gather.8.cloned.1.call-start = ((), (), s32[]{:S(2)}) async-start(), calls=%async_computation.3 | async-start | bytes 2359296 | tf_op jit(solution)/shard_map/all_gather | solution.py:10
  27.1 21.7 %collective-permute-start = (bf16[1,4,2,16,3072]{4,3,2,1,0:T(8,128)(2,1)S(1)}, bf16[1,4,2,16,3072]{4,3,2,1,0:T(8,128)(2,1)S(1)}, u32[]{:S(2)}, u32[]{:S(2)}) collective-permute-start(bf16[1,4,2,16,3072]{4,3,2,1,0:T(8,128)(2,1)S(1)} %bitcast.187), channel_id=1, source_target_pairs={{0,4},{4,8},{8,12},{12,16},{16,20},{20,24},{24,28},{28,0},{1,5},{5... | collective-permute-start | bytes 2359304 | tf_op jit(solution)/shard_map/ppermute | solution.py:160
  48.9 122.5 %copy-start.1 = (bf16[1,4,2,16,3072]{4,3,2,1,0:T(8,128)(2,1)}, bf16[1,4,2,16,3072]{4,3,2,1,0:T(8,128)(2,1)S(1)}, u32[]{:S(2)}) copy-start(bf16[1,4,2,16,3072]{4,3,2,1,0:T(8,128)(2,1)S(1)} %collective-permute-done) | copy-start | bytes 2359300
  48.9 26.1 %collective-permute-start.1 = (bf16[1,4,2,16,3072]{4,3,2,1,0:T(8,128)(2,1)S(1)}, bf16[1,4,2,16,3072]{4,3,2,1,0:T(8,128)(2,1)S(1)}, u32[]{:S(2)}, u32[]{:S(2)}) collective-permute-start(bf16[1,4,2,16,3072]{4,3,2,1,0:T(8,128)(2,1)S(1)} %collective-permute-done), channel_id=1, source_target_pairs={{0,4},{4,8},{8,12},{12,16},{16,20},{20,24},{24,28},{28,0},{1,5},{5... | collective-permute-start | bytes 2359304 | tf_op jit(solution)/shard_map/ppermute | solution.py:160
  52.8 209.0 %all-gather.6.cloned.1.call-start = ((), (), s32[]{:S(2)}) async-start(), calls=%async_computation.2 | async-start | bytes 2359296 | tf_op jit(solution)/shard_map/all_gather | solution.py:10
  75.0 76.5 %copy-start.3 = (bf16[1,4,2,16,3072]{4,3,2,1,0:T(8,128)(2,1)}, bf16[1,4,2,16,3072]{4,3,2,1,0:T(8,128)(2,1)S(1)}, u32[]{:S(2)}) copy-start(bf16[1,4,2,16,3072]{4,3,2,1,0:T(8,128)(2,1)S(1)} %collective-permute-done.1) | copy-start | bytes 2359300
  75.0 20.0 %collective-permute-start.2 = (bf16[1,4,2,16,3072]{4,3,2,1,0:T(8,128)(2,1)S(1)}, bf16[1,4,2,16,3072]{4,3,2,1,0:T(8,128)(2,1)S(1)}, u32[]{:S(2)}, u32[]{:S(2)}) collective-permute-start(bf16[1,4,2,16,3072]{4,3,2,1,0:T(8,128)(2,1)S(1)} %collective-permute-done.1), channel_id=1, source_target_pairs={{0,4},{4,8},{8,12},{12,16},{16,20},{20,24},{24,28},{28,0},{1,5},{5... | collective-permute-start | bytes 2359304 | tf_op jit(solution)/shard_map/ppermute | solution.py:160
  95.0 0.9 copy-start.5
  95.9 37.2 %collective-permute-start.3 = (bf16[1,4,2,16,3072]{4,3,2,1,0:T(8,128)(2,1)S(1)}, bf16[1,4,2,16,3072]{4,3,2,1,0:T(8,128)(2,1)S(1)}, u32[]{:S(2)}, u32[]{:S(2)}) collective-permute-start(bf16[1,4,2,16,3072]{4,3,2,1,0:T(8,128)(2,1)S(1)} %collective-permute-done.2), channel_id=1, source_target_pairs={{0,4},{4,8},{8,12},{12,16},{16,20},{20,24},{24,28},{28,0},{1,5},{5... | collective-permute-start | bytes 2359304 | tf_op jit(solution)/shard_map/ppermute | solution.py:160
  133.1 0.9 copy-start.7
  134.0 17.5 %collective-permute-start.4 = (bf16[1,4,2,16,3072]{4,3,2,1,0:T(8,128)(2,1)S(1)}, bf16[1,4,2,16,3072]{4,3,2,1,0:T(8,128)(2,1)}, u32[]{:S(2)}, u32[]{:S(2)}) collective-permute-start(bf16[1,4,2,16,3072]{4,3,2,1,0:T(8,128)(2,1)S(1)} %collective-permute-done.3), channel_id=1, source_target_pairs={{0,4},{4,8},{8,12},{12,16},{16,20},{20,24},{24,28},{28,0},{1,5},{5... | collective-permute-start | bytes 2359304 | tf_op jit(solution)/shard_map/ppermute | solution.py:160
  151.5 18.7 %collective-permute-start.5 = (bf16[1,4,2,16,3072]{4,3,2,1,0:T(8,128)(2,1)}, bf16[1,4,2,16,3072]{4,3,2,1,0:T(8,128)(2,1)}, u32[]{:S(2)}, u32[]{:S(2)}) collective-permute-start(bf16[1,4,2,16,3072]{4,3,2,1,0:T(8,128)(2,1)} %collective-permute-done.4), channel_id=1, source_target_pairs={{0,4},{4,8},{8,12},{12,16},{16,20},{20,24},{24,28},{28,0},{1,5},{5... | collective-permute-start | bytes 2359304 | tf_op jit(solution)/shard_map/ppermute | solution.py:160
  170.2 25.7 %collective-permute-start.6 = (bf16[1,4,2,16,3072]{4,3,2,1,0:T(8,128)(2,1)}, bf16[1,4,2,16,3072]{4,3,2,1,0:T(8,128)(2,1)}, u32[]{:S(2)}, u32[]{:S(2)}) collective-permute-start(bf16[1,4,2,16,3072]{4,3,2,1,0:T(8,128)(2,1)} %collective-permute-done.5), channel_id=1, source_target_pairs={{0,4},{4,8},{8,12},{12,16},{16,20},{20,24},{24,28},{28,0},{1,5},{5... | collective-permute-start | bytes 2359304 | tf_op jit(solution)/shard_map/ppermute | solution.py:160
  171.3 288.2 %all-reduce.3.cloned.1.call-start = ((), (), s32[]{:S(2)}) async-start(), calls=%async_computation.4 | async-start | bytes 12582912
  194.5 5.2 %copy-start.8 = (bf16[1,4,2,16,3072]{4,3,2,1,0:T(8,128)(2,1)S(1)}, bf16[1,4,2,16,3072]{4,3,2,1,0:T(8,128)(2,1)}, u32[]{:S(2)}) copy-start(bf16[1,4,2,16,3072]{4,3,2,1,0:T(8,128)(2,1)} %copy-done.7) | copy-start | bytes 2359300
  194.5 5.3 %copy-start.6 = (bf16[1,4,2,16,3072]{4,3,2,1,0:T(8,128)(2,1)S(1)}, bf16[1,4,2,16,3072]{4,3,2,1,0:T(8,128)(2,1)}, u32[]{:S(2)}) copy-start(bf16[1,4,2,16,3072]{4,3,2,1,0:T(8,128)(2,1)} %copy-done.5) | copy-start | bytes 2359300
  194.5 5.3 %copy-start.4 = (bf16[1,4,2,16,3072]{4,3,2,1,0:T(8,128)(2,1)S(1)}, bf16[1,4,2,16,3072]{4,3,2,1,0:T(8,128)(2,1)}, u32[]{:S(2)}) copy-start(bf16[1,4,2,16,3072]{4,3,2,1,0:T(8,128)(2,1)} %copy-done.3) | copy-start | bytes 2359300
  194.5 5.4 %copy-start.2 = (bf16[1,4,2,16,3072]{4,3,2,1,0:T(8,128)(2,1)S(1)}, bf16[1,4,2,16,3072]{4,3,2,1,0:T(8,128)(2,1)}, u32[]{:S(2)}) copy-start(bf16[1,4,2,16,3072]{4,3,2,1,0:T(8,128)(2,1)} %copy-done.1) | copy-start | bytes 2359300
  272.6 196.1 %copy-start.9 = (bf16[128,8,128]{0,2,1:T(8,128)(2,1)S(1)}, bf16[128,8,128]{0,2,1:T(8,128)(2,1)}, u32[]{:S(2)}) copy-start(bf16[128,8,128]{0,2,1:T(8,128)(2,1)} %fusion.54) | copy-start | bytes 786436
  462.3 15.1 %all-to-all-start.1 = ((bf16[4,2,16,3072]{3,2,1,0:T(8,128)(2,1)}), bf16[4,2,16,3072]{3,2,1,0:T(8,128)(2,1)S(1)}, u32[]{:S(2)}, u32[]{:S(2)}) async-start(bf16[4,2,16,3072]{3,2,1,0:T(8,128)(2,1)} %copy.168), calls=%async_computation.1 | async-start | bytes 1572864 | tf_op jit(solution)/shard_map/all_to_all | solution.py:169
Sparse Core Ops, SparseCore 0:
  52.9 77.3 all-gather.7
  171.4 49.8 all-gather.5
  251.2 208.2 all-reduce.2
